TPU v7x, 512 devices: a whole 4x4x16 slice. The times are simulated.
512 devices in a mesh: lon: 16 (over z), lat: 8 (over x_lo, y), ch: 4 (over x_hi, core).
Axes of the slice: x: 4 (x_hi: 2, x_lo: 2; x = x_hi * 2 + x_lo), y: 4, z: 16, core: 2. Of those that a mesh axis runs over, the one named last changes fastest.
Arguments:
- ocean_state: bfloat16 [300, 256, 2048], P('ch', 'lat', 'lon'), may hold values from -6 to 6
- land_mask: int32 [256, 2048], P('lat', 'lon'), may hold values 0 or 1
- out_grad: bfloat16 [300, 256, 2048], P('ch', 'lat', 'lon'), may hold values from -6 to 6
- swath_offset: int32 [8, 16, 512], P('lat', 'lon'), may hold values from 0 to 4095
- swath_value: float32 [8, 16, 512], P('lat', 'lon'), may hold values from -8 to 8
- depth_kernel: float32 [3, 3, 300], P(None, None, 'ch'), may hold values from -2.5 to 2.5
- expand_weight: bfloat16 [300, 600], P(None, 'ch'), may hold values from -0.375 to 0.375
- expand_bias: float32 [600], P('ch'), may hold values from -3 to 3
- project_weight: bfloat16 [600, 300], P('ch'), may hold values from -0.25 to 0.25
Outputs:
- state_grad: bfloat16 [300, 256, 2048], P('ch', 'lat', 'lon')
- expand_grad: float32 [300, 600], P(None, 'ch')
- project_grad: float32 [600, 300], P('ch')
- bias_grad: float32 [600], P('ch')
- kernel_grad: float32 [3, 3, 300], P(None, None, 'ch')
Inputs may be any that keep to these rules, and one draw needn't show every extreme that they name: `swath_offset`: position of a swath point in row-major order over the 32 x 128 cells of its device's block.
All inputs are finite; a program needn't handle non-finite values. No bound on the sum of `land_mask` on one device may be relied on, other than what follows from the above.
Results may differ from a plain program's by a relative error of at most 0.014.
Values may be sent and summed in bfloat16 or wider, within the bound.
A program may use at most 64 MiB of HBM per device.

v0:
```python
import math
import jax
import jax.numpy as jnp
from jax import lax
from jax.sharding import PartitionSpec as P

DILATION_STEP = 2


def with_halo(block, sides, width):
    for axis, dim in sides:
        count = lax.axis_size(axis)
        forward = [(i, i + 1) for i in range(count - 1)]
        forward.append((count - 1, 0))
        backward = [(target, source) for source, target in forward]
        low = lax.ppermute(
            lax.slice_in_dim(block, block.shape[dim] - width, None, axis=dim), axis, forward
        )
        high = lax.ppermute(lax.slice_in_dim(block, 0, width, axis=dim), axis, backward)
        block = jnp.concatenate([low, block, high], axis=dim)
    return block


def extend(ocean_field):
    count_of_rows = ocean_field.shape[1]
    column_count = ocean_field.shape[2]
    halo_padded = with_halo(ocean_field, (("lon", 2), ("lat", 1)), DILATION_STEP)
    uppermost_rows = ocean_field[:, count_of_rows - DILATION_STEP :, :]
    gathered = lax.all_gather(uppermost_rows, "lon", axis=2, tiled=True)
    seam_mirrored = gathered[:, ::-1, ::-1]
    seam_mirrored = jnp.concatenate(
        [seam_mirrored[:, :, -DILATION_STEP:], seam_mirrored, seam_mirrored[:, :, :DILATION_STEP]],
        axis=2,
    )
    northern_border = lax.dynamic_slice_in_dim(
        seam_mirrored, lax.axis_index("lon") * column_count, column_count + 2 * DILATION_STEP, 2
    )
    latitude_index = lax.axis_index("lat")
    southern_boundary = halo_padded[:, :DILATION_STEP, :]
    southern_border = jnp.where(
        latitude_index == 0, jnp.zeros_like(southern_boundary), southern_boundary
    )
    northern_border = jnp.where(
        latitude_index == lax.axis_size("lat") - 1,
        northern_border,
        halo_padded[:, count_of_rows + DILATION_STEP :, :],
    )
    return jnp.concatenate(
        [
            southern_border,
            halo_padded[:, DILATION_STEP : count_of_rows + DILATION_STEP, :],
            northern_border,
        ],
        axis=1,
    )


def on_device(
    ocean_state,
    land_mask,
    out_grad,
    swath_offset,
    swath_value,
    depth_kernel,
    expand_weight,
    expand_bias,
    project_weight,
):
    channels_per_shard = ocean_state.shape[0]
    count_of_rows = ocean_state.shape[1]
    column_count = ocean_state.shape[2]
    cells = count_of_rows * column_count
    scale = 1.0 / math.sqrt(
        count_of_rows * lax.axis_size("lat") * column_count * lax.axis_size("lon")
    )
    mask_float = land_mask.astype(jnp.float32)[None]
    masked = ocean_state * land_mask.astype(jnp.bfloat16)[None]
    state_pad = extend(masked)
    forward = jnp.zeros((channels_per_shard, count_of_rows, column_count), jnp.float32)
    for row_offset in range(3):
        for column_offset in range(3):
            kernel_window = state_pad[
                :,
                DILATION_STEP * row_offset : DILATION_STEP * row_offset + count_of_rows,
                DILATION_STEP * column_offset : DILATION_STEP * column_offset + column_count,
            ]
            forward = forward + depth_kernel[row_offset, column_offset][
                :, None, None
            ] * kernel_window.astype(jnp.float32)
    conv_out = forward.astype(jnp.bfloat16)
    swath = (
        jnp.zeros((cells,), jnp.float32).at[swath_offset.reshape(-1)].add(swath_value.reshape(-1))
    )
    first_group = jnp.where(lax.axis_index("ch") == 0, 1.0, 0.0).astype(jnp.float32)
    cotan = (
        out_grad.astype(jnp.float32)
        .at[0]
        .add(first_group * swath.reshape(count_of_rows, column_count))
    )
    cotan = (cotan * mask_float).astype(jnp.bfloat16)
    conv_all, cotan_all = (
        lax.all_gather(conv_out, "ch", axis=0, tiled=True),
        lax.all_gather(cotan, "ch", axis=0, tiled=True),
    )
    conv_flat = conv_all.reshape(conv_all.shape[0], cells)
    cotan_flat = cotan_all.reshape(cotan_all.shape[0], cells)
    hidden = (
        jnp.dot(expand_weight.T, conv_flat, preferred_element_type=jnp.float32)
        + expand_bias[:, None]
    )
    activ, gelu_back = jax.vjp(jax.nn.gelu, hidden)
    act_grad = jnp.dot(project_weight, cotan_flat, preferred_element_type=jnp.float32)
    pre_grad = gelu_back(act_grad)[0].astype(jnp.bfloat16)
    project_part = (
        jnp.dot(activ.astype(jnp.bfloat16), cotan_flat.T, preferred_element_type=jnp.float32)
        * scale
    )
    expand_part = jnp.dot(conv_flat, pre_grad.T, preferred_element_type=jnp.float32) * scale
    bias_part = jnp.sum(pre_grad.astype(jnp.float32), axis=1) * scale
    summed = lax.psum_scatter(
        jnp.dot(expand_weight, pre_grad, preferred_element_type=jnp.float32).astype(jnp.bfloat16),
        "ch",
        scatter_dimension=0,
        tiled=True,
    )
    conv_grad = summed.reshape(channels_per_shard, count_of_rows, column_count)
    grad_pad = extend(conv_grad)
    grad_float = conv_grad.astype(jnp.float32)
    kernel_rows = []
    swapped_axes = jnp.zeros((channels_per_shard, count_of_rows, column_count), jnp.float32)
    for row_offset in range(3):
        kernel_cols = []
        for column_offset in range(3):
            kernel_window = state_pad[
                :,
                DILATION_STEP * row_offset : DILATION_STEP * row_offset + count_of_rows,
                DILATION_STEP * column_offset : DILATION_STEP * column_offset + column_count,
            ]
            kernel_cols.append(jnp.sum(grad_float * kernel_window.astype(jnp.float32), axis=(1, 2)))
            reverse_row = DILATION_STEP * (2 - row_offset)
            reverse_column = DILATION_STEP * (2 - column_offset)
            back_window = grad_pad[
                :,
                reverse_row : reverse_row + count_of_rows,
                reverse_column : reverse_column + column_count,
            ]
            swapped_axes = swapped_axes + depth_kernel[row_offset, column_offset][
                :, None, None
            ] * back_window.astype(jnp.float32)
        kernel_rows.append(jnp.stack(kernel_cols, axis=0))
    kernel_part = jnp.stack(kernel_rows, axis=0) * scale
    fold_adjustment = jnp.zeros((channels_per_shard, DILATION_STEP, column_count), jnp.float32)
    for column_offset in range(3):
        reverse_column = DILATION_STEP * (2 - column_offset)
        rim_window = grad_pad[
            :,
            count_of_rows + DILATION_STEP : count_of_rows + 2 * DILATION_STEP,
            reverse_column : reverse_column + column_count,
        ]
        weight_change = depth_kernel[2, 2 - column_offset] - depth_kernel[0, column_offset]
        fold_adjustment = fold_adjustment + weight_change[:, None, None] * rim_window.astype(
            jnp.float32
        )
    at_top = lax.axis_index("lat") == lax.axis_size("lat") - 1
    swapped_axes = swapped_axes.at[:, count_of_rows - DILATION_STEP :, :].add(
        jnp.where(at_top, fold_adjustment, jnp.zeros_like(fold_adjustment))
    )
    state_grad = (mask_float * (cotan.astype(jnp.float32) + swapped_axes)).astype(jnp.bfloat16)
    expand_grad, project_grad, bias_grad, kernel_grad = lax.psum(
        (expand_part, project_part, bias_part, kernel_part), ("lon", "lat")
    )
    return (state_grad, expand_grad, project_grad, bias_grad, kernel_grad)


def solution(mesh):
    return jax.shard_map(
        on_device,
        mesh=mesh,
        in_specs=(
            P("ch", "lat", "lon"),
            P("lat", "lon"),
            P("ch", "lat", "lon"),
            P("lat", "lon", None),
            P("lat", "lon", None),
            P(None, None, "ch"),
            P(None, "ch"),
            P("ch"),
            P("ch", None),
        ),
        out_specs=(
            P("ch", "lat", "lon"),
            P(None, "ch"),
            P("ch", None),
            P("ch"),
            P(None, None, "ch"),
        ),
        check_vma=False,
    )
```

profile of v0, /device:TPU:4, one launch (start us, length us, event | category | flops | bytes accessed | tf_op | source)
XLA Modules:
  0.0 1292.7 jit_solution(13573045520863102719)
XLA Ops:
  10.0 3.4 scatter_custom_fusion
  16.0 11.4 collective-permute-start.1
  30.1 32.5 %all_gather.13 = bf16[75,2,2048]{2,1,0:T(2,128)(2,1)S(1)} all-gather(bf16[75,2,128]{2,1,0:T(2,128)(2,1)S(1)} %slice.277), channel_id=1, replica_groups=mesh['lon'=16,'lat'=8,'ch'=4] {'lon'}, dimensions={2}, use_global_device_ids=true | all-gather | bytes 652800 | tf_op jit(solution)/shard_map/all_gather | solution.py:29
  65.4 3.5 collective-permute-start.2
  69.5 5.5 rev.6
  75.7 4.0 concatenate.54
  79.7 4.5 collective-permute-start.3
  87.2 2.4 maximum_maximum_fusion
  91.3 4.1 fusion.19
  98.1 2.1 pad.67
  101.5 23.7 %all-gather.5.cloned.1.call-done = bf16[300,32,128]{2,1,0:T(8,128)(2,1)} async-done(((bf16[75,32,128]{2,1,0:T(8,128)(2,1)}), bf16[300,32,128]{2,1,0:T(8,128)(2,1)}) %all-gather.5.cloned.1.call-update) | async-done | bytes 2457616 | tf_op jit(solution)/shard_map/all_gather | solution.py:102
  125.2 2.1 pad.68
  129.4 1.9 fusion.34
  131.3 2.5 convert_reduce_fusion
  136.7 2.2 fusion.2
  138.9 31.6 %fusion = bf16[80,4096]{1,0:T(8,128)(2,1)} fusion(bf16[300,4096]{1,0:T(8,128)(2,1)S(1)} %fusion.2), kind=kCustom, calls=%all-reduce-scatter | all-reduce-scatter fusion | flops 1310721 | bytes 3115008
  171.4 1.9 collective-permute-start.8
  173.9 5.3 collective-permute-done.8
  179.2 6.0 concatenate.62
  186.9 4.9 fusion.28
  192.2 34.5 %all_gather.15 = bf16[75,2,2048]{2,1,0:T(2,128)(2,1)S(1)} all-gather(bf16[75,2,128]{2,1,0:T(2,128)(2,1)S(1)} %slice.285), channel_id=1, replica_groups=mesh['lon'=16,'lat'=8,'ch'=4] {'lon'}, dimensions={2}, use_global_device_ids=true | all-gather | bytes 652800 | tf_op jit(solution)/shard_map/all_gather | solution.py:29
  228.3 3.0 collective-permute-start.5
  231.3 2.8 collective-permute-start.4
  234.4 3.8 collective-permute-done.4
  240.7 3.2 collective-permute-start.7
  244.0 5.5 rev.7
  250.1 4.0 concatenate.57
  254.2 311.0 %all-reduce.2 = (f32[150]{0:T(256)}, f32[3,3,75]{2,1,0:T(4,128)}) all-reduce(f32[150]{0:T(256)S(1)} %copy-done.33, f32[3,3,75]{2,1,0:T(4,128)S(1)} %maximum_multiply_fusion), channel_id=1, replica_groups=mesh['lon'=16,'lat'=8,'ch'=4] {'lon','lat'}, use_global_device_ids=true, to_apply=%region_5.6 | all-reduce | flops 825 | bytes 6600 | tf_op jit(solution)/shard_map/psum | solution.py:169
  567.2 4.3 collective-permute-done.6
  572.6 2.4 pad_maximum_fusion.1
  575.2 3.4 fusion.24
  580.2 702.8 %all-reduce.6.cloned.1.call-done = (f32[300,150]{0,1:T(8,128)}, f32[150,300]{1,0:T(8,128)}) async-done(((f32[300,150]{0,1:T(8,128)}, f32[150,300]{1,0:T(8,128)}), (f32[300,150]{0,1:T(8,128)}, f32[150,300]{1,0:T(8,128)})) %all-reduce.6.cloned.1.call-update) | async-done | bytes 360016 | tf_op jit(solution)/shard_map/psum | solution.py:169
  (158 shorter events, 41.2 us)
Async XLA Ops:
  7.2 121.4 %copy-start = (bf16[300,150]{0,1:T(8,128)(2,1)S(1)}, bf16[300,150]{0,1:T(8,128)(2,1)}, u32[]{:S(2)}) copy-start(bf16[300,150]{0,1:T(8,128)(2,1)} %param.19) | copy-start | bytes 270004
  7.2 91.0 %all-gather.3.cloned.1.call-start = ((), (), s32[]{:S(2)}) async-start(), calls=%async_computation | async-start | bytes 3072000 | tf_op jit(solution)/shard_map/all_gather | solution.py:103
  14.4 110.8 %all-gather.5.cloned.1.call-start = ((), (), s32[]{:S(2)}) async-start(), calls=%async_computation.1 | async-start | bytes 3072000 | tf_op jit(solution)/shard_map/all_gather | solution.py:102
  16.0 47.9 %collective-permute-start.1 = (bf16[75,32,2]{0,1,2:T(8,128)(2,1)S(1)}, bf16[75,32,2]{0,1,2:T(8,128)(2,1)S(1)}, u32[]{:S(2)}, u32[]{:S(2)}) collective-permute-start(bf16[75,32,2]{0,1,2:T(8,128)(2,1)S(1)} %copy.31), channel_id=1, source_target_pairs={{32,0},{64,32},{96,64},{128,96},{160,128},{192,160},{224,192},{256... | collective-permute-start | bytes 28808 | tf_op jit(solution)/shard_map/ppermute | solution.py:19
  28.2 34.6 %collective-permute-start = (bf16[75,32,2]{0,1,2:T(8,128)(2,1)S(1)}, bf16[75,32,2]{0,1,2:T(8,128)(2,1)S(1)}, u32[]{:S(2)}, u32[]{:S(2)}) collective-permute-start(bf16[75,32,2]{0,1,2:T(8,128)(2,1)S(1)} %copy.30), channel_id=1, source_target_pairs={{0,32},{32,64},{64,96},{96,128},{128,160},{160,192},{192,224},{224... | collective-permute-start | bytes 28808 | tf_op jit(solution)/shard_map/ppermute | solution.py:16
  63.8 25.8 %copy-start.5 = (bf16[75,32,2]{2,1,0:T(8,128)(2,1)}, bf16[75,32,2]{2,1,0:T(8,128)(2,1)S(1)}, u32[]{:S(2)}) copy-start(bf16[75,32,2]{2,1,0:T(8,128)(2,1)S(1)} %copy.32) | copy-start | bytes 28804
  64.9 24.7 %copy-start.7 = (bf16[75,32,2]{2,1,0:T(8,128)(2,1)}, bf16[75,32,2]{2,1,0:T(8,128)(2,1)S(1)}, u32[]{:S(2)}) copy-start(bf16[75,32,2]{2,1,0:T(8,128)(2,1)S(1)} %copy.33) | copy-start | bytes 28804
  65.4 18.8 %collective-permute-start.2 = (bf16[75,2,132]{2,1,0:T(2,128)(2,1)S(1)}, bf16[75,2,132]{2,1,0:T(2,128)(2,1)}, u32[]{:S(2)}, u32[]{:S(2)}) collective-permute-start(bf16[75,2,132]{2,1,0:T(2,128)(2,1)S(1)} %get-tuple-element.51), channel_id=1, source_target_pairs={{0,4},{4,8},{8,12},{12,16},{16,20},{20,24},{24,28},{28,0},{1,5},{5... | collective-permute-start | bytes 118808 | tf_op jit(solution)/shard_map/ppermute | solution.py:16
  69.5 20.2 %copy-start.14 = (f32[75]{0:T(128)}, f32[75]{0:T(128)S(1)}, u32[]{:S(2)}) copy-start(f32[75]{0:T(128)S(1)} %get-tuple-element.72) | copy-start | bytes 904
  69.5 20.2 %copy-start.16 = (f32[75]{0:T(128)}, f32[75]{0:T(128)S(1)}, u32[]{:S(2)}) copy-start(f32[75]{0:T(128)S(1)} %get-tuple-element.73) | copy-start | bytes 904
  69.5 20.2 %copy-start.18 = (f32[75]{0:T(128)}, f32[75]{0:T(128)S(1)}, u32[]{:S(2)}) copy-start(f32[75]{0:T(128)S(1)} %get-tuple-element.74) | copy-start | bytes 904
  69.5 20.2 %copy-start.20 = (f32[75]{0:T(128)}, f32[75]{0:T(128)S(1)}, u32[]{:S(2)}) copy-start(f32[75]{0:T(128)S(1)} %get-tuple-element.75) | copy-start | bytes 904
  69.5 20.2 %copy-start.22 = (f32[75]{0:T(128)}, f32[75]{0:T(128)S(1)}, u32[]{:S(2)}) copy-start(f32[75]{0:T(128)S(1)} %get-tuple-element.76) | copy-start | bytes 904
  69.5 20.2 %copy-start.24 = (f32[75]{0:T(128)}, f32[75]{0:T(128)S(1)}, u32[]{:S(2)}) copy-start(f32[75]{0:T(128)S(1)} %get-tuple-element.77) | copy-start | bytes 904
  79.7 6.5 collective-permute-start.3
  95.4 1187.5 %all-reduce.6.cloned.1.call-start = ((), (), s32[]{:S(2)}) async-start(), calls=%async_computation.2 | async-start | bytes 933888 | tf_op jit(solution)/shard_map/psum | solution.py:169
  171.4 7.8 collective-permute-start.8
  173.3 13.4 %copy-start.8 = (bf16[75,32,2]{2,1,0:T(8,128)(2,1)S(1)}, bf16[75,32,2]{2,1,0:T(8,128)(2,1)}, u32[]{:S(2)}) copy-start(bf16[75,32,2]{2,1,0:T(8,128)(2,1)} %copy-done.7) | copy-start | bytes 28804
  192.1 42.1 %copy-start.34 = (f32[75]{0:T(128)S(1)}, f32[75]{0:T(128)}, u32[]{:S(2)}) copy-start(f32[75]{0:T(128)} %get-tuple-element.35) | copy-start | bytes 904
  192.1 42.1 %copy-start.35 = (f32[75]{0:T(128)S(1)}, f32[75]{0:T(128)}, u32[]{:S(2)}) copy-start(f32[75]{0:T(128)} %get-tuple-element.36) | copy-start | bytes 904
  192.1 42.1 %copy-start.36 = (f32[75]{0:T(128)S(1)}, f32[75]{0:T(128)}, u32[]{:S(2)}) copy-start(f32[75]{0:T(128)} %get-tuple-element.37) | copy-start | bytes 904
  192.1 42.1 %copy-start.37 = (f32[75]{0:T(128)S(1)}, f32[75]{0:T(128)}, u32[]{:S(2)}) copy-start(f32[75]{0:T(128)} %get-tuple-element.56) | copy-start | bytes 904
  192.1 42.1 %copy-start.38 = (f32[75]{0:T(128)S(1)}, f32[75]{0:T(128)}, u32[]{:S(2)}) copy-start(f32[75]{0:T(128)} %get-tuple-element.57) | copy-start | bytes 904
  192.1 42.1 %copy-start.39 = (f32[75]{0:T(128)S(1)}, f32[75]{0:T(128)}, u32[]{:S(2)}) copy-start(f32[75]{0:T(128)} %get-tuple-element.58) | copy-start | bytes 904
  192.1 42.1 %copy-start.43 = (f32[75]{0:T(128)S(1)}, f32[75]{0:T(128)}, u32[]{:S(2)}) copy-start(f32[75]{0:T(128)} %get-tuple-element.53) | copy-start | bytes 904
  192.2 42.1 %copy-start.44 = (f32[75]{0:T(128)S(1)}, f32[75]{0:T(128)}, u32[]{:S(2)}) copy-start(f32[75]{0:T(128)} %get-tuple-element.54) | copy-start | bytes 904
  192.2 42.1 %copy-start.45 = (f32[75]{0:T(128)S(1)}, f32[75]{0:T(128)}, u32[]{:S(2)}) copy-start(f32[75]{0:T(128)} %get-tuple-element.55) | copy-start | bytes 904
  228.3 10.9 collective-permute-start.5
  231.3 6.8 collective-permute-start.4
  240.7 326.4 %collective-permute-start.7 = (bf16[75,2,132]{2,1,0:T(2,128)(2,1)S(1)}, bf16[75,2,132]{2,1,0:T(2,128)(2,1)}, u32[]{:S(2)}, u32[]{:S(2)}) collective-permute-start(bf16[75,2,132]{2,1,0:T(2,128)(2,1)S(1)} %get-tuple-element.48), channel_id=1, source_target_pairs={{0,4},{4,8},{8,12},{12,16},{16,20},{20,24},{24,28},{28,0},{1,5},{5... | collective-permute-start | bytes 118808 | tf_op jit(solution)/shard_map/ppermute | solution.py:16
  244.0 10.2 copy-start.33
  565.2 6.3 collective-permute-start.6
  (27 other events, 74.9 us)
Sparse Core Ops, SparseCore 0:
  14.5 38.0 all-gather.2
  95.5 29.6 all-gather.4
  173.5 1109.3 all-reduce.5
where the time goes:
time: 1290 us
  waiting for transfers between devices  742 us (58%)
  blocking collectives  410 us (32%)
  local copies, waits for them, and re-layouts  52.1 us (4%)
  starting transfers between devices  34.4 us (3%)
  other arithmetic  30.2 us (2%)
  between operations  15.4 us (1%)
    psum x1, waiting for transfers between devices, on_device(): lax.psum((expand_part, project_part, bias_part, kernel_part), ('lon', 'la...  703 us
    psum x1, blocking collectives, on_device(): lax.psum((expand_part, project_part, bias_part, kernel_part), ('lon', 'la...  311 us
    all_gather x2, blocking collectives, extend(): gathered = lax.all_gather(uppermost_rows, 'lon', axis=2, tiled=True)  67 us
    unnamed x1, blocking collectives  31.6 us
  transfers between devices with their start and end apart: 12, of which 6 were waited for; matrix products, arithmetic and copies ran while one was open for 5% of the time, Pallas kernels for 0%

commit v1 on v0

--- a/solution.py
+++ b/solution.py
@@ -167,7 +167,7 @@
     )
     state_grad = (mask_float * (cotan.astype(jnp.float32) + swapped_axes)).astype(jnp.bfloat16)
     expand_grad, project_grad, bias_grad, kernel_grad = lax.psum(
-        (expand_part, project_part, bias_part, kernel_part), ("lon", "lat")
+        lax.psum((expand_part, project_part, bias_part, kernel_part), "lon"), "lat"
     )
     return (state_grad, expand_grad, project_grad, bias_grad, kernel_grad)
 

time: 1290 us -> 415 us (0.32)
  waiting for transfers between devices: 742 us -> 122 us
  blocking collectives: 410 us -> 146 us
    psum x1 -> x2, waiting for transfers between devices: 703 us -> 83 us  [the longest x1 83 us: on_device(): lax.psum(lax.psum((expand_part, project_part, bias_part, kernel_part), 'l...]
    psum x1 -> x2, blocking collectives: 311 us -> 47.2 us  [the longest x1 27.8 us: on_device(): lax.psum((expand_part, project_part, bias_part, kernel_part), 'lon')]
  transfers between devices with their start and end apart: 12 -> 13, of which waited for: 6 -> 6; matrix products, arithmetic and copies ran while one was open for 5% -> 16% of each run, Pallas kernels for 0% -> 0%
where the time goes in v1:
time: 415 us; the launch traced here: 413 us
  blocking collectives  146 us (35%)
  waiting for transfers between devices  122 us (29%)
  local copies, waits for them, and re-layouts  52.1 us (13%)
  starting transfers between devices  34.9 us (8%)
  other arithmetic  33.6 us (8%)
  between operations  15.4 us (4%)
  matrix products  9.26 us (2%)
    psum x1, waiting for transfers between devices, on_device(): lax.psum(lax.psum((expand_part, project_part, bias_part, kernel_part), 'l...  83 us
    all_gather x2, blocking collectives, extend(): gathered = lax.all_gather(uppermost_rows, 'lon', axis=2, tiled=True)  67.4 us
    unnamed x1, blocking collectives  31.6 us
    psum x1, blocking collectives, on_device(): lax.psum((expand_part, project_part, bias_part, kernel_part), 'lon')  27.8 us
    all_gather x1, waiting for transfers between devices, on_device(): lax.all_gather(conv_out, 'ch', axis=0, tiled=True)  23.7 us
    unnamed x105, local copies, waits for them, and re-layouts  23.1 us
    ppermute x4, starting transfers between devices, with_halo(): lax.ppermute(lax.slice_in_dim(block, 0, width, axis=dim), axis, backward)  20.5 us
    psum x1, blocking collectives, on_device(): lax.psum(lax.psum((expand_part, project_part, bias_part, kernel_part), 'l...  19.4 us
  transfers between devices with their start and end apart: 13, of which 6 were waited for; matrix products, arithmetic and copies ran while one was open for 16% of the time, Pallas kernels for 0%

profile of v1, /device:TPU:4, one launch (start us, length us, event | category | flops | bytes accessed | tf_op | source)
XLA Modules:
  0.0 413.3 jit_solution(2876506250483872609)
XLA Ops:
  10.0 3.4 scatter_custom_fusion
  16.0 11.4 %collective-permute-start.1 = (bf16[75,32,2]{0,1,2:T(8,128)(2,1)S(1)}, bf16[75,32,2]{0,1,2:T(8,128)(2,1)S(1)}, u32[]{:S(2)}, u32[]{:S(2)}) collective-permute-start(bf16[75,32,2]{0,1,2:T(8,128)(2,1)S(1)} %copy.31), channel_id=1, source_target_pairs={{32,0},{64,32},{96,64},{128,96},{160,128},{192,160},{224,192},{256... | collective-permute-start | bytes 28808 | tf_op jit(solution)/shard_map/ppermute | solution.py:19
  30.1 32.5 %all_gather.13 = bf16[75,2,2048]{2,1,0:T(2,128)(2,1)S(1)} all-gather(bf16[75,2,128]{2,1,0:T(2,128)(2,1)S(1)} %slice.277), channel_id=1, replica_groups=mesh['lon'=16,'lat'=8,'ch'=4] {'lon'}, dimensions={2}, use_global_device_ids=true | all-gather | bytes 652800 | tf_op jit(solution)/shard_map/all_gather | solution.py:29
  65.4 3.5 collective-permute-start.2
  69.5 5.5 %rev.6 = bf16[75,2,2048]{2,1,0:T(2,128)(2,1)S(1)} reverse(bf16[75,2,2048]{2,1,0:T(2,128)(2,1)S(1)} %all_gather.13), dimensions={1,2} | reverse | bytes 1228800 | tf_op jit(solution)/shard_map/rev | solution.py:30
  75.7 4.0 concatenate.54
  79.7 4.5 %collective-permute-start.3 = (bf16[75,2,132]{2,1,0:T(2,128)(2,1)S(1)}, bf16[75,2,132]{2,1,0:T(2,128)(2,1)S(1)}, u32[]{:S(2)}, u32[]{:S(2)}) collective-permute-start(bf16[75,2,132]{2,1,0:T(2,128)(2,1)S(1)} %get-tuple-element.56), channel_id=1, source_target_pairs={{4,0},{8,4},{12,8},{16,12},{20,16},{24,20},{28,24},{0,28},{5,1},{9... | collective-permute-start | bytes 118808 | tf_op jit(solution)/shard_map/ppermute | solution.py:19
  87.2 2.4 maximum_maximum_fusion
  91.3 4.1 fusion.19
  98.1 2.1 pad.67
  101.5 23.7 %all-gather.5.cloned.1.call-done = bf16[300,32,128]{2,1,0:T(8,128)(2,1)} async-done(((bf16[75,32,128]{2,1,0:T(8,128)(2,1)}), bf16[300,32,128]{2,1,0:T(8,128)(2,1)}) %all-gather.5.cloned.1.call-update) | async-done | bytes 2457616 | tf_op jit(solution)/shard_map/all_gather | solution.py:102
  125.2 2.1 pad.68
  131.3 2.5 convert_reduce_fusion
  136.7 2.2 fusion.2
  138.9 31.6 %fusion = bf16[80,4096]{1,0:T(8,128)(2,1)} fusion(bf16[300,4096]{1,0:T(8,128)(2,1)S(1)} %fusion.2), kind=kCustom, calls=%all-reduce-scatter | all-reduce-scatter fusion | flops 1310721 | bytes 3115008
  174.0 5.2 %collective-permute-done.8 = bf16[15,4096]{1,0:T(8,128)(2,1)S(1)} collective-permute-done((bf16[15,4096]{1,0:T(8,128)(2,1)S(1)}, bf16[15,4096]{1,0:T(8,128)(2,1)S(1)}, u32[]{:S(2)}, u32[]{:S(2)}) %collective-permute-start.8) | collective-permute-done | bytes 122912
  179.2 6.0 %concatenate.62 = bf16[95,4096]{1,0:T(8,128)(2,1)} concatenate(bf16[15,4096]{1,0:T(8,128)(2,1)S(1)} %collective-permute-done.8, bf16[80,4096]{1,0:T(8,128)(2,1)} %fusion), dimensions={0} | concatenate | bytes 1556480
  186.9 4.9 %fusion.28 = (f32[75]{0:T(128)}, f32[75]{0:T(128)}, f32[75]{0:T(128)}, f32[75]{0:T(128)}, f32[75]{0:T(128)}, /*index=5*/f32[75]{0:T(128)}, f32[75]{0:T(128)}, f32[75]{0:T(128)}, f32[75]{0:T(128)}) fusion(bf16[75,32,128]{2,1,0:T(8,128)(2,1)S(1)} %broadcast_multiply_fusion, bf16[75,32,2]{2,1,0:T(8,128)(2,1)S(1)} %copy-done.6, ...), kind=kLoop, calls=%fused_computation.58 | loop fusion | flops 10444125 | bytes 4937100 | tf_op jit(solution)/shard_map/reduce_sum | solution.py:139
  192.2 34.9 %all_gather.15 = bf16[75,2,2048]{2,1,0:T(2,128)(2,1)S(1)} all-gather(bf16[75,2,128]{2,1,0:T(2,128)(2,1)S(1)} %slice.285), channel_id=1, replica_groups=mesh['lon'=16,'lat'=8,'ch'=4] {'lon'}, dimensions={2}, use_global_device_ids=true | all-gather | bytes 652800 | tf_op jit(solution)/shard_map/all_gather | solution.py:29
  228.8 2.8 collective-permute-start.5
  231.5 3.1 collective-permute-start.4
  234.8 3.6 collective-permute-done.4
  240.9 3.7 collective-permute-start.7
  244.7 5.5 %rev.7 = bf16[75,2,2048]{2,1,0:T(2,128)(2,1)S(1)} reverse(bf16[75,2,2048]{2,1,0:T(2,128)(2,1)S(1)} %all_gather.15), dimensions={1,2} | reverse | bytes 1228800 | tf_op jit(solution)/shard_map/rev | solution.py:30
  250.8 4.0 concatenate.57
  254.8 27.8 %all-reduce.2 = (f32[150]{0:T(256)S(1)}, f32[3,3,75]{2,1,0:T(4,128)S(1)}) all-reduce(f32[150]{0:T(256)S(1)} %copy-done.33, f32[3,3,75]{2,1,0:T(4,128)S(1)} %maximum_multiply_fusion), channel_id=1, replica_groups=mesh['lon'=16,'lat'=8,'ch'=4] {'lon'}, use_global_device_ids=true, to_apply=%region_7.8 | all-reduce | flops 825 | bytes 6600 | tf_op jit(solution)/shard_map/psum | solution.py:170
  282.7 19.4 %all-reduce.4 = (f32[150]{0:T(256)}, f32[3,3,75]{2,1,0:T(4,128)}) all-reduce(f32[150]{0:T(256)S(1)} %get-tuple-element.41, f32[3,3,75]{2,1,0:T(4,128)S(1)} %get-tuple-element.42), channel_id=1, replica_groups=mesh['lon'=16,'lat'=8,'ch'=4] {'lat'}, use_global_device_ids=true, to_apply=%region_8.9 | all-reduce | flops 825 | bytes 6600 | tf_op jit(solution)/shard_map/psum | solution.py:169
  304.1 4.3 %collective-permute-done.6 = bf16[75,2,132]{2,1,0:T(2,128)(2,1)S(1)} collective-permute-done((bf16[75,2,132]{2,1,0:T(2,128)(2,1)S(1)}, bf16[75,2,132]{2,1,0:T(2,128)(2,1)S(1)}, u32[]{:S(2)}, u32[]{:S(2)}) %collective-permute-start.6) | collective-permute-done | bytes 39632 | tf_op jit(solution)/shard_map/ppermute | solution.py:19
  309.5 2.4 pad_maximum_fusion.1
  312.1 4.1 fusion.24
  318.2 2.3 multiply_convert_fusion.2
  320.5 83.0 %all-reduce.11.cloned.1.call-done = (f32[300,150]{0,1:T(8,128)}, f32[150,300]{1,0:T(8,128)}) async-done(((f32[300,150]{0,1:T(8,128)}, f32[150,300]{1,0:T(8,128)}), (f32[300,150]{0,1:T(8,128)}, f32[150,300]{1,0:T(8,128)})) %all-reduce.11.cloned.1.call-update) | async-done | bytes 360016 | tf_op jit(solution)/shard_map/psum | solution.py:169
  (162 shorter events, 45.6 us)
Async XLA Ops:
  7.2 121.4 %copy-start = (bf16[300,150]{0,1:T(8,128)(2,1)S(1)}, bf16[300,150]{0,1:T(8,128)(2,1)}, u32[]{:S(2)}) copy-start(bf16[300,150]{0,1:T(8,128)(2,1)} %param.19) | copy-start | bytes 270004
  7.2 91.0 %all-gather.3.cloned.1.call-start = ((), (), s32[]{:S(2)}) async-start(), calls=%async_computation | async-start | bytes 3072000 | tf_op jit(solution)/shard_map/all_gather | solution.py:103
  14.4 110.8 %all-gather.5.cloned.1.call-start = ((), (), s32[]{:S(2)}) async-start(), calls=%async_computation.1 | async-start | bytes 3072000 | tf_op jit(solution)/shard_map/all_gather | solution.py:102
  16.0 47.9 %collective-permute-start.1 = (bf16[75,32,2]{0,1,2:T(8,128)(2,1)S(1)}, bf16[75,32,2]{0,1,2:T(8,128)(2,1)S(1)}, u32[]{:S(2)}, u32[]{:S(2)}) collective-permute-start(bf16[75,32,2]{0,1,2:T(8,128)(2,1)S(1)} %copy.31), channel_id=1, source_target_pairs={{32,0},{64,32},{96,64},{128,96},{160,128},{192,160},{224,192},{256... | collective-permute-start | bytes 28808 | tf_op jit(solution)/shard_map/ppermute | solution.py:19
  28.2 34.6 %collective-permute-start = (bf16[75,32,2]{0,1,2:T(8,128)(2,1)S(1)}, bf16[75,32,2]{0,1,2:T(8,128)(2,1)S(1)}, u32[]{:S(2)}, u32[]{:S(2)}) collective-permute-start(bf16[75,32,2]{0,1,2:T(8,128)(2,1)S(1)} %copy.30), channel_id=1, source_target_pairs={{0,32},{32,64},{64,96},{96,128},{128,160},{160,192},{192,224},{224... | collective-permute-start | bytes 28808 | tf_op jit(solution)/shard_map/ppermute | solution.py:16
  63.8 25.8 %copy-start.5 = (bf16[75,32,2]{2,1,0:T(8,128)(2,1)}, bf16[75,32,2]{2,1,0:T(8,128)(2,1)S(1)}, u32[]{:S(2)}) copy-start(bf16[75,32,2]{2,1,0:T(8,128)(2,1)S(1)} %copy.32) | copy-start | bytes 28804
  64.9 24.7 %copy-start.7 = (bf16[75,32,2]{2,1,0:T(8,128)(2,1)}, bf16[75,32,2]{2,1,0:T(8,128)(2,1)S(1)}, u32[]{:S(2)}) copy-start(bf16[75,32,2]{2,1,0:T(8,128)(2,1)S(1)} %copy.33) | copy-start | bytes 28804
  65.4 18.8 %collective-permute-start.2 = (bf16[75,2,132]{2,1,0:T(2,128)(2,1)S(1)}, bf16[75,2,132]{2,1,0:T(2,128)(2,1)}, u32[]{:S(2)}, u32[]{:S(2)}) collective-permute-start(bf16[75,2,132]{2,1,0:T(2,128)(2,1)S(1)} %get-tuple-element.55), channel_id=1, source_target_pairs={{0,4},{4,8},{8,12},{12,16},{16,20},{20,24},{24,28},{28,0},{1,5},{5... | collective-permute-start | bytes 118808 | tf_op jit(solution)/shard_map/ppermute | solution.py:16
  69.5 20.2 %copy-start.14 = (f32[75]{0:T(128)}, f32[75]{0:T(128)S(1)}, u32[]{:S(2)}) copy-start(f32[75]{0:T(128)S(1)} %get-tuple-element.76) | copy-start | bytes 904
  69.5 20.2 %copy-start.16 = (f32[75]{0:T(128)}, f32[75]{0:T(128)S(1)}, u32[]{:S(2)}) copy-start(f32[75]{0:T(128)S(1)} %get-tuple-element.77) | copy-start | bytes 904
  69.5 20.2 %copy-start.18 = (f32[75]{0:T(128)}, f32[75]{0:T(128)S(1)}, u32[]{:S(2)}) copy-start(f32[75]{0:T(128)S(1)} %get-tuple-element.78) | copy-start | bytes 904
  69.5 20.2 %copy-start.20 = (f32[75]{0:T(128)}, f32[75]{0:T(128)S(1)}, u32[]{:S(2)}) copy-start(f32[75]{0:T(128)S(1)} %get-tuple-element.79) | copy-start | bytes 904
  69.5 20.2 %copy-start.22 = (f32[75]{0:T(128)}, f32[75]{0:T(128)S(1)}, u32[]{:S(2)}) copy-start(f32[75]{0:T(128)S(1)} %get-tuple-element.80) | copy-start | bytes 904
  69.5 20.2 %copy-start.24 = (f32[75]{0:T(128)}, f32[75]{0:T(128)S(1)}, u32[]{:S(2)}) copy-start(f32[75]{0:T(128)S(1)} %get-tuple-element.81) | copy-start | bytes 904
  79.7 6.5 %collective-permute-start.3 = (bf16[75,2,132]{2,1,0:T(2,128)(2,1)S(1)}, bf16[75,2,132]{2,1,0:T(2,128)(2,1)S(1)}, u32[]{:S(2)}, u32[]{:S(2)}) collective-permute-start(bf16[75,2,132]{2,1,0:T(2,128)(2,1)S(1)} %get-tuple-element.56), channel_id=1, source_target_pairs={{4,0},{8,4},{12,8},{16,12},{20,16},{24,20},{28,24},{0,28},{5,1},{9... | collective-permute-start | bytes 118808 | tf_op jit(solution)/shard_map/ppermute | solution.py:19
  95.4 220.8 %all-reduce.9.cloned.1.call-start = ((), (), s32[]{:S(2)}) async-start(), calls=%async_computation.2 | async-start | bytes 933888 | tf_op jit(solution)/shard_map/psum | solution.py:170
  171.4 7.8 %collective-permute-start.8 = (bf16[15,4096]{1,0:T(8,128)(2,1)S(1)}, bf16[15,4096]{1,0:T(8,128)(2,1)S(1)}, u32[]{:S(2)}, u32[]{:S(2)}) collective-permute-start(bf16[15,4096]{1,0:T(8,128)(2,1)S(1)} %slice.298), channel_id=1, source_target_pairs={{0,1},{1,2},{2,3},{4,5},{5,6},{6,7},{8,9},{9,10},{10,11},{12,13},{... | collective-permute-start | bytes 368648
  173.3 13.4 %copy-start.8 = (bf16[75,32,2]{2,1,0:T(8,128)(2,1)S(1)}, bf16[75,32,2]{2,1,0:T(8,128)(2,1)}, u32[]{:S(2)}) copy-start(bf16[75,32,2]{2,1,0:T(8,128)(2,1)} %copy-done.7) | copy-start | bytes 28804
  173.4 230.1 %all-reduce.11.cloned.1.call-start = ((), (), s32[]{:S(2)}) async-start(), calls=%async_computation.3 | async-start | bytes 933888 | tf_op jit(solution)/shard_map/psum | solution.py:169
  192.1 42.5 %copy-start.34 = (f32[75]{0:T(128)S(1)}, f32[75]{0:T(128)}, u32[]{:S(2)}) copy-start(f32[75]{0:T(128)} %get-tuple-element.35) | copy-start | bytes 904
  192.1 42.5 %copy-start.35 = (f32[75]{0:T(128)S(1)}, f32[75]{0:T(128)}, u32[]{:S(2)}) copy-start(f32[75]{0:T(128)} %get-tuple-element.36) | copy-start | bytes 904
  192.1 42.5 %copy-start.36 = (f32[75]{0:T(128)S(1)}, f32[75]{0:T(128)}, u32[]{:S(2)}) copy-start(f32[75]{0:T(128)} %get-tuple-element.37) | copy-start | bytes 904
  192.1 42.5 %copy-start.37 = (f32[75]{0:T(128)S(1)}, f32[75]{0:T(128)}, u32[]{:S(2)}) copy-start(f32[75]{0:T(128)} %get-tuple-element.60) | copy-start | bytes 904
  192.1 42.5 %copy-start.38 = (f32[75]{0:T(128)S(1)}, f32[75]{0:T(128)}, u32[]{:S(2)}) copy-start(f32[75]{0:T(128)} %get-tuple-element.61) | copy-start | bytes 904
  192.1 42.5 %copy-start.39 = (f32[75]{0:T(128)S(1)}, f32[75]{0:T(128)}, u32[]{:S(2)}) copy-start(f32[75]{0:T(128)} %get-tuple-element.62) | copy-start | bytes 904
  192.1 42.5 %copy-start.43 = (f32[75]{0:T(128)S(1)}, f32[75]{0:T(128)}, u32[]{:S(2)}) copy-start(f32[75]{0:T(128)} %get-tuple-element.57) | copy-start | bytes 904
  192.2 42.5 %copy-start.44 = (f32[75]{0:T(128)S(1)}, f32[75]{0:T(128)}, u32[]{:S(2)}) copy-start(f32[75]{0:T(128)} %get-tuple-element.58) | copy-start | bytes 904
  192.2 42.5 %copy-start.45 = (f32[75]{0:T(128)S(1)}, f32[75]{0:T(128)}, u32[]{:S(2)}) copy-start(f32[75]{0:T(128)} %get-tuple-element.59) | copy-start | bytes 904
  228.8 10.7 %collective-permute-start.5 = (bf16[75,32,2]{0,1,2:T(8,128)(2,1)S(1)}, bf16[75,32,2]{0,1,2:T(8,128)(2,1)S(1)}, u32[]{:S(2)}, u32[]{:S(2)}) collective-permute-start(bf16[75,32,2]{0,1,2:T(8,128)(2,1)S(1)} %copy.37), channel_id=1, source_target_pairs={{32,0},{64,32},{96,64},{128,96},{160,128},{192,160},{224,192},{256... | collective-permute-start | bytes 28808 | tf_op jit(solution)/shard_map/ppermute | solution.py:19
  231.5 6.8 %collective-permute-start.4 = (bf16[75,32,2]{0,1,2:T(8,128)(2,1)S(1)}, bf16[75,32,2]{0,1,2:T(8,128)(2,1)S(1)}, u32[]{:S(2)}, u32[]{:S(2)}) collective-permute-start(bf16[75,32,2]{0,1,2:T(8,128)(2,1)S(1)} %copy.36), channel_id=1, source_target_pairs={{0,32},{32,64},{64,96},{96,128},{128,160},{160,192},{192,224},{224... | collective-permute-start | bytes 28808 | tf_op jit(solution)/shard_map/ppermute | solution.py:16
  240.9 63.1 %collective-permute-start.7 = (bf16[75,2,132]{2,1,0:T(2,128)(2,1)S(1)}, bf16[75,2,132]{2,1,0:T(2,128)(2,1)}, u32[]{:S(2)}, u32[]{:S(2)}) collective-permute-start(bf16[75,2,132]{2,1,0:T(2,128)(2,1)S(1)} %get-tuple-element.52), channel_id=1, source_target_pairs={{0,4},{4,8},{8,12},{12,16},{16,20},{20,24},{24,28},{28,0},{1,5},{5... | collective-permute-start | bytes 118808 | tf_op jit(solution)/shard_map/ppermute | solution.py:16
  302.1 6.3 %collective-permute-start.6 = (bf16[75,2,132]{2,1,0:T(2,128)(2,1)S(1)}, bf16[75,2,132]{2,1,0:T(2,128)(2,1)S(1)}, u32[]{:S(2)}, u32[]{:S(2)}) collective-permute-start(bf16[75,2,132]{2,1,0:T(2,128)(2,1)S(1)} %get-tuple-element.51), channel_id=1, source_target_pairs={{4,0},{8,4},{12,8},{16,12},{20,16},{24,20},{28,24},{0,28},{5,1},{9... | collective-permute-start | bytes 118808 | tf_op jit(solution)/shard_map/ppermute | solution.py:19
  (28 other events, 89.7 us)
Sparse Core Ops, SparseCore 0:
  14.5 38.0 all-gather.2
  95.5 29.6 all-gather.4
  173.5 138.7 all-reduce.8
  316.3 87.1 all-reduce.10
